TPU v7x, 32 devices: a whole 2x2x4 slice. The times are simulated.
32 devices in a mesh: elem: 16 (over z, x, core), mode: 2 (over y).
Axes of the slice: x: 2, y: 2, z: 4, core: 2. Of those that a mesh axis runs over, the one named last changes fastest.
Arguments:
- velocity: float32 [1024, 128, 128], P(None, ('elem', 'mode')), may hold values from -6 to 6
- previous: float32 [1024, 128, 128], P('mode', 'elem'), may hold values from -6 to 6
- derivative: float32 [128, 128], replicated, may hold values from -0.5 to 0.5
- stiffness: float32 [128, 128], replicated, as said below
- coupling: float32 [4, 128, 128], replicated, may hold values from -0.25 to 0.25
- reaction: float32 [128], P('elem'), may hold values from 0.5 to 4
- axial_weight: float32 [128], P('elem'), may hold values from 0.5 to 4
- neighbours: int32 [128, 4], P('elem'), may hold values from -1 to 127, as said below
Outputs:
- solution: float32 [1024, 128, 128], P('mode', 'elem')
Inputs may be any that keep to these rules, and one draw needn't show every extreme that they name: `stiffness`: symmetric with a positive diagonal. `neighbours`: elements lie on a grid of 2 rows, periodic along the rows, and 4 columns a group of 8 elements, groups in order along the columns with walls at both ends. A group's first 2 elements form its first column and its last 2 its last column; a neighbour in another group is in the next or previous group, among its first or last 2 elements.
All inputs are finite; a program needn't handle non-finite values.
Results may differ from a plain program's by a relative error of at most 0.0001.
Values sent between devices are 32-bit elements; how exact they have to be, the bound alone decides.
A program may use at most 128 MiB of HBM per device.

v0:
```python
import functools
import math

import jax
import jax.numpy as jnp
import ml_dtypes
import numpy as np
from jax import lax
from jax.experimental import pallas as pl
from jax.experimental.pallas import tpu as pltpu
from jax.sharding import PartitionSpec as P

dt_step = 0.5
first_weight = 0.7
second_weight = 1.1
CHUNKS = 8
LAG = 2
MESH = pl.DeviceIdType.MESH
bf16 = jnp.bfloat16
f32 = jnp.float32


def dft_tables(planes, modes):
    half = planes // 2
    rows = np.arange(planes)
    waves = np.where(rows <= half, rows, rows - half)
    phase = (waves[:, None] * np.arange(half)[None, :]) % planes
    angles = 2.0 * math.pi / planes * phase
    table = np.where((rows <= half)[:, None], np.cos(angles), -np.sin(angles)) * planes ** (-0.5)
    table = table.reshape(modes, planes // modes // 2, 2, half).transpose(0, 2, 1, 3)
    high = table.astype(ml_dtypes.bfloat16)
    low = (table - high.astype(np.float64)).astype(ml_dtypes.bfloat16)
    return np.stack([high, low])


def split(values):
    high = values.astype(bf16)
    low = (values - high.astype(f32)).astype(bf16)
    return high, low


def kernel(
    modes, groups, planes, elems, group_elems, rows, nodes,
    vel_hbm, prev_hbm, table_hbm, der_hbm, stiff_hbm, coup_hbm, reac, axial, near,
    out_hbm,
    vel, prev, table, der, stiff, coup, w_slope, w_apply, folded, sent, rhs, rims, first,
    halo_prev, halo_first, pairs, staged, outv,
    load_sem, y_send, y_recv, p_send, p_recv, f_send, f_recv, out_sem,
):
    half = planes // 2
    rim = group_elems // 4
    count = rows // CHUNKS
    me = lax.axis_index("mode")
    group = lax.axis_index("elem")
    zero_slot = group_elems + 2 * rim

    loads = [
        pltpu.make_async_copy(src, dst, load_sem.at[i])
        for i, (src, dst) in enumerate(
            [
                (prev_hbm, prev), (vel_hbm, vel), (der_hbm, der), (table_hbm, table),
                (stiff_hbm, stiff), (coup_hbm, coup),
            ]
        )
    ]
    for load in loads:
        load.start()

    barrier = pltpu.get_barrier_semaphore()
    for step in range(1, modes):
        pl.semaphore_signal(
            barrier, inc=1, device_id={"mode": lax.rem(me + step, modes)}, device_id_type=MESH
        )
    has_left = group > 0
    has_right = group < groups - 1

    @pl.when(has_left)
    def _():
        pl.semaphore_signal(barrier, inc=1, device_id={"elem": group - 1}, device_id_type=MESH)

    @pl.when(has_right)
    def _():
        pl.semaphore_signal(barrier, inc=1, device_id={"elem": group + 1}, device_id_type=MESH)

    def start_row(c):
        return (2 * (c // 2) * count + c % 2) * group_elems

    def prev_rows(c, e):
        return prev[pl.ds(start_row(c) + e, count, stride=2 * group_elems), :]

    def halo_copies(source, halo, send, recv, c):
        right = pltpu.make_async_remote_copy(
            source(c, 0), halo.at[0, c], send.at[0, c], recv.at[0, c],
            device_id={"elem": group + 1}, device_id_type=MESH,
        )
        left = pltpu.make_async_remote_copy(
            source(c, 1), halo.at[1, c], send.at[1, c], recv.at[1, c],
            device_id={"elem": group - 1}, device_id_type=MESH,
        )
        return right, left

    def prev_copies(c):
        return halo_copies(lambda c, side: rims.at[side, c], halo_prev, p_send, p_recv, c)

    def first_copies(c):
        def source(c, side):
            return first.at[c, pl.ds((group_elems - rim) * (1 - side), rim)]

        return halo_copies(source, halo_first, f_send, f_recv, c)

    def start_halo(copies):
        right, left = copies
        pl.when(has_right)(right.start)
        pl.when(has_left)(left.start)

    def wait_halo_recv(copies):
        right, left = copies
        pl.when(has_left)(right.wait_recv)
        pl.when(has_right)(left.wait_recv)

    def wait_halo_send(copies):
        right, left = copies
        pl.when(has_right)(right.wait_send)
        pl.when(has_left)(left.wait_send)

    loads[0].wait()

    def gather_rims(c, carry):
        for i in range(rim):
            rims[0, c, i] = prev_rows(c, group_elems - rim + i)
            rims[1, c, i] = prev_rows(c, i)
        return carry

    lax.fori_loop(0, CHUNKS, gather_rims, 0)
    pl.semaphore_wait(
        barrier, modes - 1 + has_left.astype(jnp.int32) + has_right.astype(jnp.int32)
    )

    def send_rims(c, carry):
        start_halo(prev_copies(c))
        return carry

    lax.fori_loop(0, CHUNKS, send_rims, 0)

    def set_weights(ref, at, matrix):
        high, low = split(matrix.T)
        for part in range(2):
            ref[pl.ds(at + part * nodes, nodes), pl.ds(0, nodes)] = high
            ref[pl.ds(at + part * nodes, nodes), pl.ds(nodes, nodes)] = low

    loads[1].wait()
    loads[2].wait()
    set_weights(w_slope, 0, der[...])

    block = min(256, half)
    for e in range(elems):
        for b in range(half // block):
            lower = vel[pl.ds(b * block * elems + e, block, stride=elems), :]
            upper = vel[pl.ds((half + b * block) * elems + e, block, stride=elems), :]
            values = jnp.concatenate([lower, upper], axis=0)
            both = jnp.dot(
                jnp.concatenate(split(values), axis=1), w_slope[...], preferred_element_type=f32
            )
            slope = both[:, :nodes] + both[:, nodes:]
            product = values - dt_step * values * slope
            lower, upper = product[:block], product[block:]
            for parity, value in enumerate((lower + upper, lower - upper)):
                high, low = split(value)
                where = (pl.ds(b * block, block), pl.ds(e * nodes, nodes))
                folded[(parity, 0) + where] = high
                folded[(parity, 1) + where] = low

    loads[3].wait()
    pairs_of_rows = CHUNKS // 2

    def transform(owner, parity):
        data_high, data_low = folded[parity, 0], folded[parity, 1]
        t_high, t_low = table[0, owner, parity], table[1, owner, parity]
        return (
            jnp.dot(t_high, data_high, preferred_element_type=f32)
            + jnp.dot(t_low, data_high, preferred_element_type=f32)
            + jnp.dot(t_high, data_low, preferred_element_type=f32)
        )

    def y_copy(step, c):
        return pltpu.make_async_remote_copy(
            sent.at[step - 1, c], rhs.at[me, c], y_send.at[step - 1, c], y_recv.at[step - 1, c],
            device_id={"mode": lax.rem(me + step, modes)}, device_id_type=MESH,
        )

    for parity in range(2):
        for step in range(1, modes):
            block_rows = transform(lax.rem(me + step, modes), parity)
            for j in range(pairs_of_rows):
                sent[step - 1, 2 * j + parity] = block_rows[j * count : (j + 1) * count]
            if parity == 0:
                y_copy(step, 0).start()

    def send_rows(c, carry):
        for step in range(1, modes):
            y_copy(step, c).start()
        return carry

    lax.fori_loop(1, CHUNKS, send_rows, 0)

    for parity in range(2):
        block_rows = transform(me, parity)
        for j in range(pairs_of_rows):
            rhs[me, 2 * j + parity] = block_rows[j * count : (j + 1) * count]

    loads[4].wait()
    loads[5].wait()
    set_weights(w_apply, 0, stiff[...])
    for f in range(4):
        set_weights(w_apply, 2 * nodes * (f + 1), coup[f])
    eye = lax.broadcasted_iota(jnp.int32, (nodes, nodes), 0) == lax.broadcasted_iota(
        jnp.int32, (nodes, nodes), 1
    )
    diagonal = jnp.sum(jnp.where(eye, stiff[...], 0.0), axis=0, keepdims=True)
    pairs[zero_slot] = jnp.zeros((count, 2 * nodes), bf16)

    def put_pair(slot, value):
        high, low = split(value)
        pairs[slot, :, pl.ds(0, nodes)] = high
        pairs[slot, :, pl.ds(nodes, nodes)] = low

    def apply(own, halo, copies, c):
        for e in range(group_elems):
            put_pair(rim + e, own(c, e))
        wait_halo_recv(copies)

        @pl.when(has_left)
        def _():
            for i in range(rim):
                put_pair(i, halo[0, c, i])

        @pl.when(has_right)
        def _():
            for i in range(rim):
                put_pair(rim + group_elems + i, halo[1, c, i])

        for e in range(group_elems):
            here = pl.ds(e * count, count)
            staged[here, pl.ds(0, 2 * nodes)] = pairs[rim + e]
            for f in range(4):
                n = near[f, e]
                slot = jnp.clip(n - group * group_elems + rim, 0, zero_slot - 1)
                slot = jnp.where(n >= 0, slot, zero_slot)
                staged[here, pl.ds(2 * nodes * (f + 1), 2 * nodes)] = pairs[slot]
        both = jnp.dot(staged[...], w_apply[...], preferred_element_type=f32)
        return both[:, :nodes] + both[:, nodes:]

    def shifts(c):
        places = lax.broadcasted_iota(jnp.int32, (count, nodes), 0)
        row = me * rows + 2 * ((c // 2) * count + places) + c % 2
        wave = jnp.where(row <= half, row, row - half).astype(f32)
        return 4.0 * (wave / half) ** 2

    def relaxed(weight, value, applied, shift, c, e):
        scaling = reac[e] + shift * axial[e]
        inverse = 1.0 / (diagonal + scaling)
        right = rhs[e // elems, c, :, pl.ds((e % elems) * nodes, nodes)]
        part = applied[e * count : (e + 1) * count]
        return value + weight * inverse * (right - (part + scaling * value))

    def first_sweep(c):
        applied = apply(prev_rows, halo_prev, prev_copies(c), c)
        for step in range(1, modes):
            y_copy(step, c).wait_recv()
        shift = shifts(c)
        for e in range(group_elems):
            first[c, e] = relaxed(first_weight, prev_rows(c, e), applied, shift, c, e)
        start_halo(first_copies(c))

    def out_copy(j):
        size = 2 * count * group_elems
        span = pl.ds(j * size, size)
        return pltpu.make_async_copy(outv.at[span], out_hbm.at[span], out_sem.at[j])

    def second_sweep(c):
        applied = apply(lambda c, e: first[c, e], halo_first, first_copies(c), c)
        shift = shifts(c)
        for e in range(group_elems):
            outv[pl.ds(start_row(c) + e, count, stride=2 * group_elems), :] = relaxed(
                second_weight, first[c, e], applied, shift, c, e
            )
        pl.when(c % 2 == 1)(lambda: out_copy(c // 2).start())

    def stage(s, carry):
        pl.when(s < CHUNKS)(lambda: first_sweep(s))
        pl.when(s >= LAG)(lambda: second_sweep(s - LAG))
        return carry

    lax.fori_loop(0, CHUNKS + LAG, stage, 0)

    def finish(c, carry):
        wait_halo_send(prev_copies(c))
        wait_halo_send(first_copies(c))
        for step in range(1, modes):
            y_copy(step, c).wait_send()
        return carry

    lax.fori_loop(0, CHUNKS, finish, 0)

    def finish_out(j, carry):
        out_copy(j).wait()
        return carry

    lax.fori_loop(0, pairs_of_rows, finish_out, 0)


def body(modes, groups, velocity, previous, derivative, stiffness, coupling, reaction, axial_weight, neighbours):
    planes, elems, nodes = velocity.shape
    rows, group_elems, _ = previous.shape
    half = planes // 2
    rim = group_elems // 4
    count = rows // CHUNKS
    tables = jnp.asarray(dft_tables(planes, modes))
    run = functools.partial(kernel, modes, groups, planes, elems, group_elems, rows, nodes)
    anywhere = pl.BlockSpec(memory_space=pl.ANY)
    scalar = pl.BlockSpec(memory_space=pltpu.SMEM)
    dma = pltpu.SemaphoreType.DMA
    out = pl.pallas_call(
        run,
        out_shape=jax.ShapeDtypeStruct((rows * group_elems, nodes), f32),
        in_specs=[anywhere] * 6 + [scalar] * 3,
        out_specs=anywhere,
        scratch_shapes=[
            pltpu.VMEM((planes * elems, nodes), f32),
            pltpu.VMEM((rows * group_elems, nodes), f32),
            pltpu.VMEM(tables.shape, bf16),
            pltpu.VMEM((nodes, nodes), f32),
            pltpu.VMEM((nodes, nodes), f32),
            pltpu.VMEM((4, nodes, nodes), f32),
            pltpu.VMEM((2 * nodes, 2 * nodes), bf16),
            pltpu.VMEM((10 * nodes, 2 * nodes), bf16),
            pltpu.VMEM((2, 2, half, elems * nodes), bf16),
            pltpu.VMEM((modes - 1, CHUNKS, count, elems * nodes), f32),
            pltpu.VMEM((modes, CHUNKS, count, elems * nodes), f32),
            pltpu.VMEM((2, CHUNKS, rim, count, nodes), f32),
            pltpu.VMEM((CHUNKS, group_elems, count, nodes), f32),
            pltpu.VMEM((2, CHUNKS, rim, count, nodes), f32),
            pltpu.VMEM((2, CHUNKS, rim, count, nodes), f32),
            pltpu.VMEM((group_elems + 2 * rim + 1, count, 2 * nodes), bf16),
            pltpu.VMEM((group_elems * count, 10 * nodes), bf16),
            pltpu.VMEM((rows * group_elems, nodes), f32),
            dma((6,)),
            dma((modes - 1, CHUNKS)),
            dma((modes - 1, CHUNKS)),
            dma((2, CHUNKS)),
            dma((2, CHUNKS)),
            dma((2, CHUNKS)),
            dma((2, CHUNKS)),
            dma((CHUNKS // 2,)),
        ],
        compiler_params=pltpu.CompilerParams(
            collective_id=0, has_side_effects=True, vmem_limit_bytes=63 * 1024 * 1024
        ),
        name="advect_helmholtz",
    )(
        velocity.reshape(planes * elems, nodes),
        previous.reshape(rows * group_elems, nodes),
        tables,
        derivative,
        stiffness,
        coupling,
        reaction,
        axial_weight,
        neighbours.T,
    )
    return out.reshape(rows, group_elems, nodes)


def solution(mesh):
    return jax.shard_map(
        functools.partial(body, mesh.shape["mode"], mesh.shape["elem"]),
        mesh=mesh,
        in_specs=(
            P(None, ("elem", "mode"), None),
            P("mode", "elem", None),
            P(),
            P(),
            P(),
            P("elem"),
            P("elem"),
            P("elem", None),
        ),
        out_specs=P("mode", "elem", None),
        check_vma=False,
    )
```

profile of v0, /device:TPU:1, one launch (start us, length us, event | category | flops | bytes accessed | tf_op | source)
XLA Modules:
  0.0 39.4 jit_solution(3869374132903958766)
XLA Ops:
  0.0 36.4 %advect_helmholtz.1 = f32[4096,128]{1,0:T(8,128)} custom-call(f32[4096,128]{1,0:T(8,128)} %bitcast.5, f32[4096,128]{1,0:T(8,128)} %bitcast.6, bf16[2,2,2,256,512]{4,3,2,1,0:T(8,128)(2,1)} %constant.2.clone.table_hbm, f32[128,128]{1,0:T(8,128)} %der_hbm.1, f32[128,128]{1,0:T(8,128)} %stiff_hbm.1, f32[4,128,128]{2,1,0:T(8,128)} %coup_hbm.1, f32[8]{0:T(128)} %reac.1, ...), custom_call_target="tpu_custom_call" | custom-call | tf_op jit(solution)/shard_map/advect_helmholtz/pallas_call | solution.py:323
  36.4 3.0 %copy.11 = f32[512,8,128]{2,1,0:T(8,128)} copy(f32[512,8,128]{2,1,0:T(8,128)} %bitcast.4) | data formatting | bytes 4194304
where the time goes:
time: 39.6 us; the launch traced here: 39.4 us
  Pallas kernels  36.4 us (92%)
  local copies, waits for them, and re-layouts  3.05 us (8%)
    pallas_call x1, Pallas kernels, body(): pl.pallas_call(run, out_shape=jax.ShapeDtypeStruct((rows * group_elems, n...  36.4 us
    unnamed x1, local copies, waits for them, and re-layouts  3.05 us

commit v1 on v0

--- a/solution.py
+++ b/solution.py
@@ -15,6 +15,8 @@
 second_weight = 1.1
 CHUNKS = 8
 LAG = 2
+vmem_bytes = 67043328
+vmem_spare = 262144
 MESH = pl.DeviceIdType.MESH
 bf16 = jnp.bfloat16
 f32 = jnp.float32
@@ -42,10 +44,10 @@
 def kernel(
     modes, groups, planes, elems, group_elems, rows, nodes,
     vel_hbm, prev_hbm, table_hbm, der_hbm, stiff_hbm, coup_hbm, reac, axial, near,
-    out_hbm,
+    outv,
     vel, prev, table, der, stiff, coup, w_slope, w_apply, folded, sent, rhs, rims, first,
-    halo_prev, halo_first, pairs, staged, outv,
-    load_sem, y_send, y_recv, p_send, p_recv, f_send, f_recv, out_sem,
+    halo_prev, halo_first, pairs, staged,
+    load_sem, lead_send, lead_recv, y_send, y_recv, p_send, p_recv, f_send, f_recv,
 ):
     half = planes // 2
     rim = group_elems // 4
@@ -58,7 +60,7 @@
         pltpu.make_async_copy(src, dst, load_sem.at[i])
         for i, (src, dst) in enumerate(
             [
-                (prev_hbm, prev), (vel_hbm, vel), (der_hbm, der), (table_hbm, table),
+                (vel_hbm, vel), (der_hbm, der), (table_hbm, table), (prev_hbm, prev),
                 (stiff_hbm, stiff), (coup_hbm, coup),
             ]
         )
@@ -122,25 +124,6 @@
         right, left = copies
         pl.when(has_right)(right.wait_send)
         pl.when(has_left)(left.wait_send)
-
-    loads[0].wait()
-
-    def gather_rims(c, carry):
-        for i in range(rim):
-            rims[0, c, i] = prev_rows(c, group_elems - rim + i)
-            rims[1, c, i] = prev_rows(c, i)
-        return carry
-
-    lax.fori_loop(0, CHUNKS, gather_rims, 0)
-    pl.semaphore_wait(
-        barrier, modes - 1 + has_left.astype(jnp.int32) + has_right.astype(jnp.int32)
-    )
-
-    def send_rims(c, carry):
-        start_halo(prev_copies(c))
-        return carry
-
-    lax.fori_loop(0, CHUNKS, send_rims, 0)
 
     def set_weights(ref, at, matrix):
         high, low = split(matrix.T)
@@ -149,11 +132,12 @@
             ref[pl.ds(at + part * nodes, nodes), pl.ds(nodes, nodes)] = low
 
     loads[1].wait()
-    loads[2].wait()
     set_weights(w_slope, 0, der[...])
+    loads[0].wait()
 
     block = min(256, half)
-    for e in range(elems):
+
+    def advect(e):
         for b in range(half // block):
             lower = vel[pl.ds(b * block * elems + e, block, stride=elems), :]
             upper = vel[pl.ds((half + b * block) * elems + e, block, stride=elems), :]
@@ -170,11 +154,13 @@
                 folded[(parity, 0) + where] = high
                 folded[(parity, 1) + where] = low
 
-    loads[3].wait()
     pairs_of_rows = CHUNKS // 2
-
-    def transform(owner, parity):
-        data_high, data_low = folded[parity, 0], folded[parity, 1]
+    lead = max(1, elems // 4)
+    lead_span = pl.ds(0, lead * nodes)
+    rest_span = pl.ds(lead * nodes, (elems - lead) * nodes)
+
+    def transform(owner, parity, span):
+        data_high, data_low = folded[parity, 0, :, span], folded[parity, 1, :, span]
         t_high, t_low = table[0, owner, parity], table[1, owner, parity]
         return (
             jnp.dot(t_high, data_high, preferred_element_type=f32)
@@ -182,17 +168,61 @@
             + jnp.dot(t_high, data_low, preferred_element_type=f32)
         )
 
+    def put_rows(ref, parity, block_rows, span):
+        for j in range(pairs_of_rows):
+            ref[2 * j + parity, :, span] = block_rows[j * count : (j + 1) * count]
+
+    def lead_copy(step):
+        return pltpu.make_async_remote_copy(
+            sent.at[step - 1, :, :, lead_span], rhs.at[me, :, :, lead_span],
+            lead_send.at[step - 1], lead_recv.at[step - 1],
+            device_id={"mode": lax.rem(me + step, modes)}, device_id_type=MESH,
+        )
+
     def y_copy(step, c):
         return pltpu.make_async_remote_copy(
-            sent.at[step - 1, c], rhs.at[me, c], y_send.at[step - 1, c], y_recv.at[step - 1, c],
+            sent.at[step - 1, c, :, rest_span], rhs.at[me, c, :, rest_span],
+            y_send.at[step - 1, c], y_recv.at[step - 1, c],
             device_id={"mode": lax.rem(me + step, modes)}, device_id_type=MESH,
         )
 
+    for e in range(lead):
+        advect(e)
+    loads[2].wait()
+    for step in range(1, modes):
+        for parity in range(2):
+            put_rows(
+                sent.at[step - 1], parity,
+                transform(lax.rem(me + step, modes), parity, lead_span), lead_span,
+            )
+    pl.semaphore_wait(
+        barrier, modes - 1 + has_left.astype(jnp.int32) + has_right.astype(jnp.int32)
+    )
+    for step in range(1, modes):
+        lead_copy(step).start()
+
+    loads[3].wait()
+
+    def gather_rims(c, carry):
+        for i in range(rim):
+            rims[0, c, i] = prev_rows(c, group_elems - rim + i)
+            rims[1, c, i] = prev_rows(c, i)
+        return carry
+
+    lax.fori_loop(0, CHUNKS, gather_rims, 0)
+    def send_rims(c, carry):
+        start_halo(prev_copies(c))
+        return carry
+
+    lax.fori_loop(0, CHUNKS, send_rims, 0)
+    for e in range(lead, elems):
+        advect(e)
     for parity in range(2):
         for step in range(1, modes):
-            block_rows = transform(lax.rem(me + step, modes), parity)
-            for j in range(pairs_of_rows):
-                sent[step - 1, 2 * j + parity] = block_rows[j * count : (j + 1) * count]
+            put_rows(
+                sent.at[step - 1], parity,
+                transform(lax.rem(me + step, modes), parity, rest_span), rest_span,
+            )
             if parity == 0:
                 y_copy(step, 0).start()
 
@@ -203,10 +233,9 @@
 
     lax.fori_loop(1, CHUNKS, send_rows, 0)
 
+    whole_span = pl.ds(0, elems * nodes)
     for parity in range(2):
-        block_rows = transform(me, parity)
-        for j in range(pairs_of_rows):
-            rhs[me, 2 * j + parity] = block_rows[j * count : (j + 1) * count]
+        put_rows(rhs.at[me], parity, transform(me, parity, whole_span), whole_span)
 
     loads[4].wait()
     loads[5].wait()
@@ -268,14 +297,12 @@
         for step in range(1, modes):
             y_copy(step, c).wait_recv()
         shift = shifts(c)
-        for e in range(group_elems):
+        outer = [*range(rim), *range(group_elems - rim, group_elems)]
+        for e in outer:
             first[c, e] = relaxed(first_weight, prev_rows(c, e), applied, shift, c, e)
         start_halo(first_copies(c))
-
-    def out_copy(j):
-        size = 2 * count * group_elems
-        span = pl.ds(j * size, size)
-        return pltpu.make_async_copy(outv.at[span], out_hbm.at[span], out_sem.at[j])
+        for e in range(rim, group_elems - rim):
+            first[c, e] = relaxed(first_weight, prev_rows(c, e), applied, shift, c, e)
 
     def second_sweep(c):
         applied = apply(lambda c, e: first[c, e], halo_first, first_copies(c), c)
@@ -284,7 +311,9 @@
             outv[pl.ds(start_row(c) + e, count, stride=2 * group_elems), :] = relaxed(
                 second_weight, first[c, e], applied, shift, c, e
             )
-        pl.when(c % 2 == 1)(lambda: out_copy(c // 2).start())
+
+    for step in range(1, modes):
+        lead_copy(step).wait_recv()
 
     def stage(s, carry):
         pl.when(s < CHUNKS)(lambda: first_sweep(s))
@@ -292,6 +321,9 @@
         return carry
 
     lax.fori_loop(0, CHUNKS + LAG, stage, 0)
+
+    for step in range(1, modes):
+        lead_copy(step).wait_send()
 
     def finish(c, carry):
         wait_halo_send(prev_copies(c))
@@ -301,12 +333,6 @@
         return carry
 
     lax.fori_loop(0, CHUNKS, finish, 0)
-
-    def finish_out(j, carry):
-        out_copy(j).wait()
-        return carry
-
-    lax.fori_loop(0, pairs_of_rows, finish_out, 0)
 
 
 def body(modes, groups, velocity, previous, derivative, stiffness, coupling, reaction, axial_weight, neighbours):
@@ -317,44 +343,47 @@
     count = rows // CHUNKS
     tables = jnp.asarray(dft_tables(planes, modes))
     run = functools.partial(kernel, modes, groups, planes, elems, group_elems, rows, nodes)
-    anywhere = pl.BlockSpec(memory_space=pl.ANY)
+    anywhere = pl.BlockSpec(memory_space=pltpu.HBM)
     scalar = pl.BlockSpec(memory_space=pltpu.SMEM)
     dma = pltpu.SemaphoreType.DMA
+    scratch = [
+        pltpu.VMEM((planes * elems, nodes), f32),
+        pltpu.VMEM((rows * group_elems, nodes), f32),
+        pltpu.VMEM(tables.shape, bf16),
+        pltpu.VMEM((nodes, nodes), f32),
+        pltpu.VMEM((nodes, nodes), f32),
+        pltpu.VMEM((4, nodes, nodes), f32),
+        pltpu.VMEM((2 * nodes, 2 * nodes), bf16),
+        pltpu.VMEM((10 * nodes, 2 * nodes), bf16),
+        pltpu.VMEM((2, 2, half, elems * nodes), bf16),
+        pltpu.VMEM((modes - 1, CHUNKS, count, elems * nodes), f32),
+        pltpu.VMEM((modes, CHUNKS, count, elems * nodes), f32),
+        pltpu.VMEM((2, CHUNKS, rim, count, nodes), f32),
+        pltpu.VMEM((CHUNKS, group_elems, count, nodes), f32),
+        pltpu.VMEM((2, CHUNKS, rim, count, nodes), f32),
+        pltpu.VMEM((2, CHUNKS, rim, count, nodes), f32),
+        pltpu.VMEM((group_elems + 2 * rim + 1, count, 2 * nodes), bf16),
+        pltpu.VMEM((group_elems * count, 10 * nodes), bf16),
+    ]
+    semaphores = [
+        dma((6,)),
+        dma((modes - 1,)),
+        dma((modes - 1,)),
+        dma((modes - 1, CHUNKS)),
+        dma((modes - 1, CHUNKS)),
+        dma((2, CHUNKS)),
+        dma((2, CHUNKS)),
+        dma((2, CHUNKS)),
+        dma((2, CHUNKS)),
+    ]
     out = pl.pallas_call(
         run,
-        out_shape=jax.ShapeDtypeStruct((rows * group_elems, nodes), f32),
+        out_shape=pltpu.VMEM((rows * group_elems, nodes), f32),
         in_specs=[anywhere] * 6 + [scalar] * 3,
-        out_specs=anywhere,
-        scratch_shapes=[
-            pltpu.VMEM((planes * elems, nodes), f32),
-            pltpu.VMEM((rows * group_elems, nodes), f32),
-            pltpu.VMEM(tables.shape, bf16),
-            pltpu.VMEM((nodes, nodes), f32),
-            pltpu.VMEM((nodes, nodes), f32),
-            pltpu.VMEM((4, nodes, nodes), f32),
-            pltpu.VMEM((2 * nodes, 2 * nodes), bf16),
-            pltpu.VMEM((10 * nodes, 2 * nodes), bf16),
-            pltpu.VMEM((2, 2, half, elems * nodes), bf16),
-            pltpu.VMEM((modes - 1, CHUNKS, count, elems * nodes), f32),
-            pltpu.VMEM((modes, CHUNKS, count, elems * nodes), f32),
-            pltpu.VMEM((2, CHUNKS, rim, count, nodes), f32),
-            pltpu.VMEM((CHUNKS, group_elems, count, nodes), f32),
-            pltpu.VMEM((2, CHUNKS, rim, count, nodes), f32),
-            pltpu.VMEM((2, CHUNKS, rim, count, nodes), f32),
-            pltpu.VMEM((group_elems + 2 * rim + 1, count, 2 * nodes), bf16),
-            pltpu.VMEM((group_elems * count, 10 * nodes), bf16),
-            pltpu.VMEM((rows * group_elems, nodes), f32),
-            dma((6,)),
-            dma((modes - 1, CHUNKS)),
-            dma((modes - 1, CHUNKS)),
-            dma((2, CHUNKS)),
-            dma((2, CHUNKS)),
-            dma((2, CHUNKS)),
-            dma((2, CHUNKS)),
-            dma((CHUNKS // 2,)),
-        ],
+        out_specs=pl.BlockSpec(memory_space=pltpu.VMEM),
+        scratch_shapes=scratch + semaphores,
         compiler_params=pltpu.CompilerParams(
-            collective_id=0, has_side_effects=True, vmem_limit_bytes=63 * 1024 * 1024
+            collective_id=0, has_side_effects=True, vmem_limit_bytes=vmem_bytes - 4 * rows * group_elems * nodes - 262144
         ),
         name="advect_helmholtz",
     )(

time: 39.6 us -> 35.9 us (0.907)
  Pallas kernels: 36.4 us -> 34.4 us
  local copies, waits for them, and re-layouts: 3.05 us -> 1.32 us
    pallas_call x1, Pallas kernels: 36.4 us -> 34.4 us  [body(): pl.pallas_call(run, out_shape=pltpu.VMEM((rows * group_elems, nodes), f32...]
    unnamed x1, local copies, waits for them, and re-layouts: 3.05 us -> 1.32 us
where the time goes in v1:
time: 35.9 us; the launch traced here: 35.7 us
  Pallas kernels  34.4 us (96%)
  local copies, waits for them, and re-layouts  1.32 us (4%)
    pallas_call x1, Pallas kernels, body(): pl.pallas_call(run, out_shape=pltpu.VMEM((rows * group_elems, nodes), f32...  34.4 us
    unnamed x1, local copies, waits for them, and re-layouts  1.32 us

profile of v1, /device:TPU:1, one launch (start us, length us, event | category | flops | bytes accessed | tf_op | source)
XLA Modules:
  0.0 35.7 jit_solution(15258563585503970235)
XLA Ops:
  0.0 34.4 %advect_helmholtz.1 = f32[4096,128]{1,0:T(8,128)S(1)} custom-call(f32[4096,128]{1,0:T(8,128)} %bitcast.5, f32[4096,128]{1,0:T(8,128)} %bitcast.6, bf16[2,2,2,256,512]{4,3,2,1,0:T(8,128)(2,1)} %constant.2.clone.table_hbm, f32[128,128]{1,0:T(8,128)} %der_hbm.1, f32[128,128]{1,0:T(8,128)} %stiff_hbm.1, f32[4,128,128]{2,1,0:T(8,128)} %coup_hbm.1, f32[8]{0:T(128)} %reac.1, ...), custom_call_target="tpu_custom_call" | custom-call | tf_op jit(solution)/shard_map/advect_helmholtz/pallas_call | solution.py:379
  34.4 1.3 %copy.11 = f32[512,8,128]{2,1,0:T(8,128)} copy(f32[512,8,128]{2,1,0:T(8,128)S(1)} %bitcast.4) | data formatting | bytes 4194304
